TPU v7x, 32 devices: a whole 2x2x4 slice. The times are simulated.
32 devices in a mesh: wide: 8 (over y, x, core), narrow: 4 (over z).
Axes of the slice: x: 2, y: 2, z: 4, core: 2. Of those that a mesh axis runs over, the one named last changes fastest.
Arguments:
- amps: float32 [1, 16, 640, 640], P(None, 'wide', 'narrow'), may hold values from -6 to 6
- cycle: float32 [16, 640, 5120], P(None, 'wide', 'narrow'), may hold values from -0.25 to 0.25
- irrep_i: int32 [1], replicated, may hold values from 0 to 7
- irrep_k: int32 [16], replicated, may hold values from 0 to 7, as said below
- irrep_j: int32 [8], replicated, may hold values from 0 to 7, as said below
- irrep_v: int32 [640], replicated, may hold values from 0 to 7, as said below
Outputs:
- cycle_term: float32 [1, 8, 640, 640], P(None, 'wide', 'narrow')
Inputs may be any that keep to these rules, and one draw needn't show every extreme that they name: `irrep_k`: nondecreasing along the orbitals, the first 0 and the last 7. `irrep_j`: nondecreasing along the orbitals, the first 0 and the last 7. `irrep_v`: nondecreasing along the orbitals, the first 0 and the last 7.
All inputs are finite; a program needn't handle non-finite values.
Results may differ from a plain program's by a relative error of at most 0.000071.
Values sent between devices are 32-bit elements; how exact they have to be, the bound alone decides.
A program may use at most 64 MiB of HBM per device.

v0:
```python
import jax
import jax.numpy as jnp
from jax import lax
from jax.sharding import PartitionSpec as P


def per_device(amps, cycle, irrep_i, irrep_k, irrep_j, irrep_v):
    wide_pos = lax.axis_index("wide")
    narrow_pos = lax.axis_index("narrow")
    wide_count = lax.axis_size("wide")
    narrow_count = lax.axis_size("narrow")
    i_total = amps.shape[0]
    k_local = amps.shape[1]
    a_local = amps.shape[2]
    v_total = amps.shape[3]
    k_total = cycle.shape[0]
    c_local = cycle.shape[1]
    b_local = v_total // narrow_count
    j_total = cycle.shape[2] // b_local
    j_local = j_total // wide_count
    cycle_four = cycle.reshape(k_total, c_local, b_local, j_total)
    k_labels = lax.dynamic_slice_in_dim(irrep_k, wide_pos * k_local, k_local)
    a_labels = lax.dynamic_slice_in_dim(irrep_v, narrow_pos * a_local, a_local)
    allowed_in = (
        irrep_i[:, None, None, None]
        ^ k_labels[None, :, None, None]
        ^ a_labels[None, None, :, None]
        ^ irrep_v[None, None, None, :]
        == 0
    )
    masked = jnp.where(allowed_in, amps, jnp.zeros_like(amps))
    moved = lax.all_to_all(masked, "wide", split_axis=3, concat_axis=1, tiled=True)
    piece = lax.all_gather(moved, "narrow", axis=2, tiled=True)
    part_sum = jnp.einsum("ikac,kcbj->iajb", piece, cycle_four, precision=lax.Precision.HIGHEST)
    terms = part_sum.reshape(piece.shape[0], piece.shape[2], j_total * b_local)
    summed = lax.psum_scatter(terms, "wide", scatter_dimension=2, tiled=True)
    summed_four = summed.reshape(i_total, v_total, j_local, b_local)
    j_labels = lax.dynamic_slice_in_dim(irrep_j, wide_pos * j_local, j_local)
    b_labels = lax.dynamic_slice_in_dim(irrep_v, narrow_pos * b_local, b_local)
    allowed_out = (
        irrep_i[:, None, None, None]
        ^ irrep_v[None, :, None, None]
        ^ j_labels[None, None, :, None]
        ^ b_labels[None, None, None, :]
        == 0
    )
    result = jnp.where(allowed_out, summed_four, jnp.zeros_like(summed_four)).reshape(
        i_total, v_total, j_local * b_local
    )
    returned = lax.all_to_all(result, "narrow", split_axis=1, concat_axis=2, tiled=True)
    spread = returned.reshape(i_total, a_local, narrow_count, j_local, b_local)
    return jnp.transpose(spread, (0, 3, 1, 2, 4)).reshape(i_total, j_local, a_local, v_total)


def solution(mesh):
    placed = (P(None, "wide", "narrow", None), P(None, "wide", "narrow"), P(), P(), P(), P())
    return jax.shard_map(
        per_device,
        mesh=mesh,
        in_specs=placed,
        out_specs=P(None, "wide", "narrow", None),
        check_vma=False,
    )
```

profile of v0, /device:TPU:0, one launch (start us, length us, event | category | flops | bytes accessed | tf_op | source)
XLA Modules:
  0.0 275.7 jit_solution(13251704546821410816)
XLA Ops:
  6.5 0.0 all-gather.2.cloned.1.call-start
  7.2 2.5 copy.21
  9.7 0.8 dynamic_slice.11
  10.5 0.7 dynamic-slice_xor_fusion
  11.2 0.1 broadcast_xor_fusion
  11.3 2.5 compare_select_fusion
  13.8 23.1 %all_to_all.33 = f32[1,2,160,640]{2,1,0,3:T(2,128)S(1)} all-to-all(f32[1,2,160,640]{2,1,0,3:T(2,128)S(1)} %compare_select_fusion), channel_id=1, replica_groups=mesh['wide'=8,'narrow'=4] {'wide'}, dimensions={3} | all-to-all | bytes 1638400 | tf_op jit(solution)/shard_map/all_to_all | solution.py:32
  36.9 2.2 copy.22
  39.0 0.0 all-gather.2.cloned.1.call-update
  39.1 0.0 all-reduce.3.cloned.1.call-start
  39.1 9.9 %copy.24 = f32[16,80,1280]{1,2,0:T(8,128)} copy(f32[16,80,1280]{2,1,0:T(8,128)} %param.7) | data formatting | bytes 13107200 | tf_op args[1]
  49.1 87.6 %all-gather.2.cloned.1.call-done = f32[1,16,640,80]{3,1,0,2:T(8,128)} async-done(((f32[1,16,160,80]{3,1,0,2:T(8,128)}), f32[1,16,640,80]{3,1,0,2:T(8,128)}) %all-gather.2.cloned.1.call-update) | async-done | bytes 3276816 | tf_op jit(solution)/shard_map/all_gather | solution.py:33
  136.7 4.5 %copy.23 = f32[1,16,640,80]{2,3,1,0:T(8,128)S(1)} copy(f32[1,16,640,80]{3,1,0,2:T(8,128)} %all-gather.2.cloned.1.call-done) | data formatting | bytes 6553600 | tf_op jit(solution)/shard_map/all_gather | solution.py:33
  141.1 23.5 %fusion = f32[640,160,8,1]{0,1,3,2:T(8,128)S(1)} fusion(f32[16,80,160,8]{1,3,2,0:T(8,128)} %bitcast.27, f32[1,16,640,80]{2,3,1,0:T(8,128)S(1)} %copy.23), kind=kOutput, calls=%fused_computation | convolution fusion | flops 12582912000 | bytes 13107200 | tf_op jit(solution)/shard_map/ikac,kcbj->iajb/dot_general | solution.py:34
  164.6 8.5 %copy.26 = f32[1,640,1280]{1,0,2:T(1,128)} copy(f32[1,640,1280]{1,2,0:T(8,128)S(1)} %bitcast.30) | data formatting | bytes 6553600 | tf_op jit(solution)/shard_map/reshape | solution.py:35
  173.1 0.0 copy-start.1
  173.1 0.0 copy-start.2
  173.1 0.0 copy-start
  173.1 0.0 all-reduce.3.cloned.1.call-update
  173.1 0.6 copy-done.1
  173.8 0.7 dynamic_slice.10
  174.4 0.0 copy-done.2
  174.4 0.7 dynamic-slice
  175.8 0.0 copy-done
  175.8 0.7 xor_xor_fusion
  176.5 66.1 %all-reduce.3.cloned.1.call-done = f32[1,640,1280]{1,0,2:T(1,128)} async-done(((f32[1,640,1280]{1,0,2:T(1,128)}), f32[1,640,1280]{1,0,2:T(1,128)}) %all-reduce.3.cloned.1.call-update) | async-done | bytes 3276816
  242.6 1.5 compare_select_fusion.1
  244.1 1.8 copy.27
  245.8 21.5 %all_to_all.34 = f32[1,640,160]{2,0,1:T(1,128)S(1)} all-to-all(f32[1,640,160]{2,0,1:T(1,128)S(1)} %copy.27), channel_id=1, replica_groups=mesh['wide'=8,'narrow'=4] {'narrow'}, dimensions={1} | all-to-all | bytes 819200 | tf_op jit(solution)/shard_map/all_to_all | solution.py:50
  267.3 0.4 copy.28
  267.8 1.1 reshape_transpose_reshape.3
Async XLA Ops:
  6.5 130.1 %all-gather.2.cloned.1.call-start = ((), (), s32[]{:S(2)}) async-start(), calls=%async_computation.2 | async-start | bytes 6553600 | tf_op jit(solution)/shard_map/all_gather | solution.py:33
  39.1 203.5 %all-reduce.3.cloned.1.call-start = ((), (), s32[]{:S(2)}) async-start(), calls=%async_computation.3 | async-start | bytes 6553600
  173.1 0.7 copy-start.1
  173.1 1.3 copy-start.2
  173.1 2.7 copy-start
Sparse Core Ops, SparseCore 0:
  39.2 97.4 all-gather.1
  173.3 69.2 all-reduce.2
where the time goes:
time: 276 us
  waiting for transfers between devices  154 us (56%)
  blocking collectives  44.7 us (16%)
  local copies, waits for them, and re-layouts  33.6 us (12%)
  matrix products  23.5 us (9%)
  between operations  14.8 us (5%)
  other arithmetic  5.46 us (2%)
    all_gather x1, waiting for transfers between devices, per_device(): piece = lax.all_gather(moved, 'narrow', axis=2, tiled=True)  87.6 us
    unnamed x3, waiting for transfers between devices  66.1 us
    dot_general x1, matrix products, per_device(): jnp.einsum('ikac,kcbj->iajb', piece, cycle_four, precision=lax.Precision....  23.5 us
    all_to_all x1, blocking collectives, per_device(): lax.all_to_all(masked, 'wide', split_axis=3, concat_axis=1, tiled=True)  23.1 us
    all_to_all x1, blocking collectives, per_device(): lax.all_to_all(result, 'narrow', split_axis=1, concat_axis=2, tiled=True)  21.5 us
    unnamed x9, local copies, waits for them, and re-layouts  13.7 us
    reshape x1, local copies, waits for them, and re-layouts, per_device(): terms = part_sum.reshape(piece.shape[0], piece.shape[2], j_total * b_local)  8.52 us
  transfers between devices with their start and end apart: 2, of which 2 were waited for; matrix products, arithmetic and copies ran while one was open for 4% of the time, Pallas kernels for 0%

commit v1 on v0

--- a/solution.py
+++ b/solution.py
@@ -1,10 +1,307 @@
+import functools
+
 import jax
 import jax.numpy as jnp
 from jax import lax
+from jax.experimental import pallas as pl
+from jax.experimental.pallas import tpu as pltpu
 from jax.sharding import PartitionSpec as P
 
-
-def per_device(amps, cycle, irrep_i, irrep_k, irrep_j, irrep_v):
+F32 = jnp.float32
+BF16 = jnp.bfloat16
+MESH = pl.DeviceIdType.MESH
+
+
+def pick(position, table):
+    value = jnp.int32(table[0])
+    for place in range(1, len(table)):
+        value = jnp.where(position == place, jnp.int32(table[place]), value)
+    return value
+
+
+def near_first(count):
+    return [sorted(range(count), key=lambda n: (abs(n - m), n)) for m in range(count)]
+
+
+def cycle_kernel(ranks, wn, nn, amps, cycle, ir_i, ir_k, ir_j, iv_col, iv_row, out,
+                 cyc, cth, ctl, amt, recv_one, xk, yb, yr, xh, xl, acc, send_a, recv_a, send_b, recv_b,
+                 send_c, recv_c, out_t,
+                 cyc_sem, s1, r1, sl, sr, ry, sa, ra, sb, rb, sc, rc):
+    w = lax.axis_index("wide")
+    m = lax.axis_index("narrow")
+    kl, al, vt = amps.shape
+    kt, cl, bj = cycle.shape
+    jt = wn
+    bl = bj // jt
+    depth = kt * cl
+    quarter = bl // 4
+    pairs = wn // 2
+    core = lax.rem(w, 2)
+    chip = w // 2
+    partner = w + 1 - 2 * core
+
+    load = pltpu.make_async_copy(cycle, cyc, cyc_sem)
+    load.start()
+
+    barrier = pltpu.get_barrier_semaphore()
+    for d in range(1, wn):
+        pl.semaphore_signal(barrier, inc=1, device_id={"wide": lax.rem(w + d, wn)}, device_id_type=MESH)
+    for d in range(1, nn):
+        pl.semaphore_signal(barrier, inc=1, device_id={"narrow": lax.rem(m + d, nn)}, device_id_type=MESH)
+
+    label_i = ir_i[0]
+    ca = iv_col[...] ^ iv_row[m]
+    for e in range(kl):
+        turned = jnp.transpose(amps[e], (1, 0))
+        kept = jnp.where(ca == (label_i ^ ir_k[w * kl + e]), turned, 0.0)
+        amt[:, e * al:(e + 1) * al] = kept
+
+    pl.semaphore_wait(barrier, wn + nn - 2)
+
+    first = []
+    for d in range(1, wn):
+        peer = lax.rem(w + d, wn)
+        copy = pltpu.make_async_remote_copy(
+            src_ref=amt.at[pl.ds(pl.multiple_of(peer * cl, 8), cl)], dst_ref=recv_one.at[w],
+            send_sem=s1.at[d], recv_sem=r1.at[d], device_id={"wide": peer}, device_id_type=MESH)
+        copy.start()
+        first.append(copy)
+    recv_one[w] = amt[pl.ds(pl.multiple_of(w * cl, 8), cl), :]
+
+    if xh.shape[1] > al:
+        xh[:, al:] = jnp.zeros((depth, xh.shape[1] - al), BF16)
+        xl[:, al:] = jnp.zeros((depth, xh.shape[1] - al), BF16)
+    load.wait()
+    cyc_rows = cyc.reshape(depth, bj)
+
+    @pl.loop(0, depth // 128)
+    def _(row):
+        here = pl.multiple_of(row * 128, 128)
+        for col in range(bj // 128):
+            block = jnp.transpose(cyc_rows[pl.ds(here, 128), col * 128:(col + 1) * 128], (1, 0))
+            high = block.astype(BF16)
+            cth[col * 128:(col + 1) * 128, pl.ds(here, 128)] = high
+            ctl[col * 128:(col + 1) * 128, pl.ds(here, 128)] = (block - high.astype(F32)).astype(BF16)
+
+    for copy in first:
+        copy.wait()
+    for src in range(wn):
+        for e in range(kl):
+            xk[src * kl + e] = recv_one[src, :, e * al:(e + 1) * al]
+
+    starts, counts = [], []
+    labels = [ir_k[k] for k in range(kt)]
+    for g in range(8):
+        below = jnp.int32(0)
+        same = jnp.int32(0)
+        for k in range(kt):
+            below = below + jnp.where(labels[k] < g, 1, 0)
+            same = same + jnp.where(labels[k] == g, 1, 0)
+        starts.append(below)
+        counts.append(same)
+    for r in range(ranks):
+        total = jnp.zeros((cl, al), F32)
+        for g in range(8):
+            value = xk[jnp.minimum(starts[g] + r, kt - 1)]
+            total = total + jnp.where(r < counts[g], value, 0.0)
+        yr[r] = total
+    yb[m] = jnp.concatenate([yr[r] for r in range(ranks)], axis=1)
+    rank_of = []
+    for k in range(kt):
+        place = jnp.int32(0)
+        for other in range(k):
+            place = place + jnp.where(labels[other] == labels[k], 1, 0)
+        rank_of.append(jnp.minimum(place, ranks - 1))
+
+    def send_right(block):
+        return pltpu.make_async_remote_copy(
+            src_ref=yb.at[block], dst_ref=yb.at[block], send_sem=sr.at[block], recv_sem=ry.at[block],
+            device_id={"narrow": jnp.minimum(m + 1, nn - 1)}, device_id_type=MESH)
+
+    def send_left(block):
+        return pltpu.make_async_remote_copy(
+            src_ref=yb.at[block], dst_ref=yb.at[block], send_sem=sl.at[block], recv_sem=ry.at[block],
+            device_id={"narrow": jnp.maximum(m - 1, 0)}, device_id_type=MESH)
+
+    @pl.when(m < nn - 1)
+    def _():
+        send_right(m).start()
+
+    @pl.when(m > 0)
+    def _():
+        send_left(m).start()
+
+    order = near_first(nn)
+    blocks = [pick(m, [order[z][t] for z in range(nn)]) for t in range(nn)]
+    c_labels = iv_col[pl.ds(pl.multiple_of(w * cl, 8), cl), :]
+
+    def stage_a_copy(t):
+        return pltpu.make_async_remote_copy(
+            src_ref=send_a.at[t], dst_ref=recv_a.at[t], send_sem=sa.at[t], recv_sem=ra.at[t],
+            device_id={"wide": partner}, device_id_type=MESH)
+
+    def stage_b_copies(t):
+        return [pltpu.make_async_remote_copy(
+            src_ref=send_b.at[t, lax.rem(chip + d, pairs)], dst_ref=recv_b.at[t, d - 1],
+            send_sem=sb.at[t, d - 1], recv_sem=rb.at[t, d - 1],
+            device_id={"wide": 2 * lax.rem(chip + d, pairs) + core}, device_id_type=MESH)
+            for d in range(1, pairs)]
+
+    def stage_c_copy(t):
+        return pltpu.make_async_remote_copy(
+            src_ref=send_c.at[t], dst_ref=recv_c.at[m], send_sem=sc.at[t], recv_sem=rc.at[m],
+            device_id={"narrow": blocks[t]}, device_id_type=MESH)
+
+    def packed(j):
+        tiles = [acc[n, pl.ds(j, bl, stride=jt), :] for n in range(acc.shape[0])]
+        value = jnp.concatenate(tiles, axis=1)[:, :al]
+        return jnp.concatenate([value[q * quarter:(q + 1) * quarter] for q in range(4)], axis=1)
+
+    def compute(t):
+        block = blocks[t]
+        if t:
+            send_left(block).wait_recv()
+
+            @pl.when((block < m) & (m < nn - 1))
+            def _():
+                send_right(block).start()
+
+            @pl.when((block > m) & (m > 0))
+            def _():
+                send_left(block).start()
+
+            for r in range(ranks):
+                yr[r] = yb[block, :, r * al:(r + 1) * al]
+        pair = c_labels ^ iv_row[block]
+        for k in range(kt):
+            value = jnp.where(pair == (label_i ^ labels[k]), yr[rank_of[k]], 0.0)
+            high = value.astype(BF16)
+            xh[k * cl:(k + 1) * cl, :al] = high
+            xl[k * cl:(k + 1) * cl, :al] = (value - high.astype(F32)).astype(BF16)
+
+        @pl.loop(0, bj // 256)
+        def _(tile):
+            rows = pl.ds(pl.multiple_of(tile * 256, 256), 256)
+            one = jnp.dot(cth[rows, :], xh[...], preferred_element_type=F32)
+            two = jnp.dot(cth[rows, :], xl[...], preferred_element_type=F32)
+            three = jnp.dot(ctl[rows, :], xh[...], preferred_element_type=F32)
+            summed = one + (two + three)
+            for n in range(acc.shape[0]):
+                acc[n, rows, :] = summed[:, n * 128:(n + 1) * 128]
+
+        for p in range(pairs):
+            send_a[t, p] = packed(2 * p + 1 - core)
+            send_b[t, p] = packed(2 * p + core)
+        stage_a_copy(t).start()
+
+    def finish_a(t):
+        stage_a_copy(t).wait()
+        for p in range(pairs):
+            send_b[t, p] = send_b[t, p] + recv_a[t, p]
+        for copy in stage_b_copies(t):
+            copy.start()
+
+    def finish_b(t):
+        for copy in stage_b_copies(t):
+            copy.wait()
+        total = send_b[t, chip]
+        for d in range(1, pairs):
+            total = total + recv_b[t, d - 1]
+        if t == 0:
+            recv_c[m] = total
+        else:
+            send_c[t] = total
+            stage_c_copy(t).start()
+
+    for t in range(nn):
+        compute(t)
+        if t >= 1:
+            finish_a(t - 1)
+        if t >= 2:
+            finish_b(t - 2)
+    finish_a(nn - 1)
+    finish_b(nn - 2)
+    finish_b(nn - 1)
+
+    for t in range(1, nn):
+        pltpu.make_async_remote_copy(
+            src_ref=send_c.at[t], dst_ref=recv_c.at[blocks[t]], send_sem=sc.at[t], recv_sem=rc.at[blocks[t]],
+            device_id={"narrow": blocks[t]}, device_id_type=MESH).wait()
+    for z in range(nn):
+        for q in range(4):
+            base = z * bl + q * quarter
+            out_t[base:base + quarter, :] = recv_c[z, :, q * al:(q + 1) * al]
+    kept = jnp.where(ca == (label_i ^ ir_j[w]), out_t[...], 0.0)
+    out[...] = jnp.transpose(kept, (1, 0))
+
+    @pl.when(m < nn - 1)
+    def _():
+        send_right(m).wait_send()
+
+    @pl.when(m > 0)
+    def _():
+        send_left(m).wait_send()
+
+    for t in range(1, nn):
+        block = blocks[t]
+
+        @pl.when((block < m) & (m < nn - 1))
+        def _():
+            send_right(block).wait_send()
+
+        @pl.when((block > m) & (m > 0))
+        def _():
+            send_left(block).wait_send()
+
+
+def packed_path(ranks, ident, amps, cycle, irrep_i, irrep_k, irrep_j, irrep_v):
+    wn = lax.axis_size("wide")
+    nn = lax.axis_size("narrow")
+    _, kl, al, vt = amps.shape
+    kt, cl, bj = cycle.shape
+    bl = bj // wn
+    depth = kt * cl
+    pairs = wn // 2
+    pack = (bl // 4, 4 * al)
+    lanes = -(-al // 128) * 128
+    vmem = pl.BlockSpec(memory_space=pltpu.VMEM)
+    smem = pl.BlockSpec(memory_space=pltpu.SMEM)
+    dma = pltpu.SemaphoreType.DMA
+    result = pl.pallas_call(
+        functools.partial(cycle_kernel, ranks, wn, nn),
+        out_shape=jax.ShapeDtypeStruct((al, vt), F32),
+        in_specs=[vmem, pl.BlockSpec(memory_space=pl.ANY), smem, smem, smem, vmem, vmem],
+        out_specs=vmem,
+        scratch_shapes=[
+            pltpu.VMEM((kt, cl, bj), F32),
+            pltpu.VMEM((bj, depth), BF16),
+            pltpu.VMEM((bj, depth), BF16),
+            pltpu.VMEM((vt, kl * al), F32),
+            pltpu.VMEM((wn, cl, kl * al), F32),
+            pltpu.VMEM((kt, cl, al), F32),
+            pltpu.VMEM((nn, cl, ranks * al), F32),
+            pltpu.VMEM((ranks, cl, al), F32),
+            pltpu.VMEM((depth, lanes), BF16),
+            pltpu.VMEM((depth, lanes), BF16),
+            pltpu.VMEM((lanes // 128, bj, 128), F32),
+            pltpu.VMEM((nn, pairs) + pack, F32),
+            pltpu.VMEM((nn, pairs) + pack, F32),
+            pltpu.VMEM((nn, pairs) + pack, F32),
+            pltpu.VMEM((nn, pairs - 1) + pack, F32),
+            pltpu.VMEM((nn,) + pack, F32),
+            pltpu.VMEM((nn,) + pack, F32),
+            pltpu.VMEM((vt, al), F32),
+            dma, dma((wn,)), dma((wn,)), dma((nn,)), dma((nn,)), dma((nn,)),
+            dma((nn,)), dma((nn,)), dma((nn, pairs - 1)), dma((nn, pairs - 1)), dma((nn,)), dma((nn,)),
+        ],
+        compiler_params=pltpu.CompilerParams(
+            collective_id=ident, has_side_effects=True, vmem_limit_bytes=56 * 1024 * 1024),
+    )(amps[0], cycle, irrep_i, irrep_k, irrep_j,
+      irrep_v.reshape(vt, 1), irrep_v.reshape(nn, 1, al))
+    return result.reshape(1, 1, al, vt)
+
+
+def general_path(amps, cycle, irrep_i, irrep_k, irrep_j, irrep_v):
     wide_pos = lax.axis_index("wide")
     narrow_pos = lax.axis_index("narrow")
     wide_count = lax.axis_size("wide")
@@ -52,6 +349,23 @@
     return jnp.transpose(spread, (0, 3, 1, 2, 4)).reshape(i_total, j_local, a_local, v_total)
 
 
+def per_device(amps, cycle, irrep_i, irrep_k, irrep_j, irrep_v):
+    wn = lax.axis_size("wide")
+    nn = lax.axis_size("narrow")
+    kt, cl, bj = cycle.shape
+    bl = amps.shape[3] // nn
+    fits = (amps.shape[0] == 1 and bj == bl * wn and wn % 2 == 0 and cl % 16 == 0 and bl % 32 == 0
+            and amps.shape[2] % 32 == 0 and bj % 256 == 0 and (kt * cl) % 128 == 0)
+    if not fits:
+        return general_path(amps, cycle, irrep_i, irrep_k, irrep_j, irrep_v)
+    most = jnp.max(jnp.sum((irrep_k[:, None] == irrep_k[None, :]).astype(jnp.int32), axis=0))
+    level = (most > 4).astype(jnp.int32) + (most > 8).astype(jnp.int32)
+    return lax.switch(
+        level,
+        [functools.partial(packed_path, 4, 0), functools.partial(packed_path, 8, 1), general_path],
+        amps, cycle, irrep_i, irrep_k, irrep_j, irrep_v)
+
+
 def solution(mesh):
     placed = (P(None, "wide", "narrow", None), P(None, "wide", "narrow"), P(), P(), P(), P())
     return jax.shard_map(

time: 276 us -> 95.6 us (0.35)
  waiting for transfers between devices: 154 us -> 0 us
  Pallas kernels: 0 us -> 74 us
  blocking collectives: 44.7 us -> 0 us
  local copies, waits for them, and re-layouts: 33.6 us -> 4.7 us
  matrix products: 23.5 us -> 0 us
  other arithmetic: 5.46 us -> 1.45 us
    all_gather x1 -> x0, waiting for transfers between devices: 87.6 us -> none  [per_device(): piece = lax.all_gather(moved, 'narrow', axis=2, tiled=True)]
    pallas_call x0 -> x1, Pallas kernels: none -> 74 us  [packed_path(): pl.pallas_call(functools.partial(cycle_kernel, ranks, wn, nn), out_shape=...]
    unnamed x3 -> x0, waiting for transfers between devices: 66.1 us -> none
    all_to_all x2 -> x0, blocking collectives: 44.7 us -> none  [the longest x1 23.1 us: per_device(): lax.all_to_all(masked, 'wide', split_axis=3, concat_axis=1, tiled=True)]
    dot_general x1 -> x0, matrix products: 23.5 us -> none  [per_device(): jnp.einsum('ikac,kcbj->iajb', piece, cycle_four, precision=lax.Precision....]
    unnamed x9 -> x1, local copies, waits for them, and re-layouts: 13.7 us -> 1.78 us
    reshape x1 -> x2, local copies, waits for them, and re-layouts: 8.52 us -> 2.92 us  [the longest x1 1.56 us: packed_path(): irrep_v.reshape(vt, 1)]
    all_gather x1 -> x0, local copies, waits for them, and re-layouts: 4.45 us -> none  [per_device(): piece = lax.all_gather(moved, 'narrow', axis=2, tiled=True)]
  transfers between devices with their start and end apart: 2 -> 0, of which waited for: 2 -> 0; matrix products, arithmetic and copies ran while one was open for 4% -> 0% of each run, Pallas kernels for 0% -> 0%
where the time goes in v1:
time: 95.6 us; the launch traced here: 95.3 us
  Pallas kernels  74 us (77%)
  between operations  14.7 us (15%)
  local copies, waits for them, and re-layouts  4.7 us (5%)
  other arithmetic  1.45 us (2%)
    pallas_call x1, Pallas kernels, packed_path(): pl.pallas_call(functools.partial(cycle_kernel, ranks, wn, nn), out_shape=...  74 us

profile of v1, /device:TPU:0, one launch (start us, length us, event | category | flops | bytes accessed | tf_op | source)
XLA Modules:
  0.0 95.3 jit_solution(7385347771156321398)
XLA Ops:
  6.5 0.8 convert_reduce_fusion
  7.4 0.6 reduce_max.9
  9.3 77.4 %conditional.1 = (f32[1,1,160,640]{3,2,1,0:T(8,128)}) conditional(s32[]{:T(128)} %clamp.3, (f32[1,2,160,640]{3,2,1,0:T(8,128)}, s32[640]{0:T(1024)}, f32[16,80,1280]{2,1,0:T(8,128)}, s32[1]{0:T(128)}, s32[16]{0:T(128)}, /*index=5*/s32[8]{0:T(128)}) %tuple.14, (f32[1,2,160,640]{3,2,1,0:T(8,128)}, s32[640]{0:T(1024)}, ...), branch_computations={%region_2.0_spmd, %region_3.0_spmd, %region_4.6_spmd} | conditional | flops 12584653824 | bytes 84404312 | solution.py:363
  9.5 1.6 %reshape.155.iv_col = s32[640,1]{1,0:T(8,128)} reshape(s32[640]{0:T(1024)} %get-tuple-element.56) | data formatting | bytes 5120 | tf_op jit(solution)/shard_map/cond/branch_1_fun/reshape | solution.py:300
  11.1 1.4 %reshape.146.iv_row = s32[4,1,160]{2,1,0:T(1,128)} reshape(s32[640]{0:T(1024)} %get-tuple-element.56) | data formatting | bytes 5120 | tf_op jit(solution)/shard_map/cond/branch_1_fun/reshape | solution.py:300
  12.5 74.0 %branch_1_fun.1 = f32[160,640]{1,0:T(8,128)} custom-call(f32[2,160,640]{2,1,0:T(8,128)} %bitcast.31, f32[16,80,1280]{2,1,0:T(8,128)} %get-tuple-element.52.cycle, s32[1]{0:T(128)} %get-tuple-element.53.ir_i, s32[16]{0:T(128)} %get-tuple-element.54.ir_k, s32[8]{0:T(128)} %get-tuple-element.55.ir_j, s32[640,1]{1,0:T(8,128)} %reshape.155.iv_col, ...), custom_call_target="tpu_custom_call" | custom-call | tf_op jit(solution)/shard_map/cond/branch_1_fun/pallas_call | solution.py:270
  86.7 1.8 %copy.56 = f32[1,1,160,640]{3,2,1,0:T(8,128)} copy(f32[1,1,160,640]{3,2,1,0:T(8,128)} %get-tuple-element.63) | data formatting | bytes 819200
